TPU v7x, 128 devices: a whole 4x4x4 slice. The times are simulated.
128 devices in a mesh: rows: 8 (over z, core), seq: 16 (over x, y).
Axes of the slice: x: 4, y: 4, z: 4, core: 2. Of those that a mesh axis runs over, the one named last changes fastest.
Arguments:
- queries: bfloat16 [4096, 4096], P('seq'), may hold values from -50 to 50
- keys: bfloat16 [4096, 4096], P('seq'), may hold values from -6 to 6
- values: bfloat16 [4096, 4096], P('seq'), may hold values from -6 to 6
- grad_out: bfloat16 [8, 4096, 4096], P('rows', 'seq'), may hold values from -6 to 6
- table: bfloat16 [33, 4096], replicated, may hold values from -6 to 6
- positions: int32 [8], P('rows'), may hold values from 0 to 4095
- residues: int32 [8], P('rows'), may hold values from 4 to 23
- tiles: int32 [32, 8], replicated, may hold values from 0 to 31, as said below
- counts: int32 [32], replicated, may hold values from 1 to 8, as said below
Outputs:
- grad_queries: bfloat16 [8, 4096, 4096], P('rows', 'seq')
- grad_keys: bfloat16 [8, 4096, 4096], P('rows', 'seq')
- grad_values: bfloat16 [8, 4096, 4096], P('rows', 'seq')
Inputs may be any that keep to these rules, and one draw needn't show every extreme that they name: `tiles`: row i lists key blocks: entry 0 is i itself, the others differ from i and from each other. Only the first counts[i] entries of row i of tiles are used; some query block uses all 8.
All inputs are finite; a program needn't handle non-finite values.
Results may differ from a plain program's by a relative error of at most 0.0085.
Values may be sent and summed in bfloat16 or wider, within the bound.
No kernel may reach another device: no remote copies, remote signals or barrier semaphores. Data moves between devices by JAX's collectives and lax.ppermute only.
A program may use at most 128 MiB of HBM per device.

v0:
```python
import math
import jax
import jax.numpy as jnp
from jax import lax
from jax.sharding import PartitionSpec as P

D_HEAD = 128
BLOCK = 128
TILES = 8


def substitute(grad_out, table, positions, residues, first_token):
    tok_count = grad_out.shape[1]
    spots = (
        jnp.arange(tok_count, dtype=jnp.int32)[None, :] + first_token == positions[:, None]
    ).astype(jnp.float32)
    picks = (jnp.arange(table.shape[0], dtype=jnp.int32)[None, :] == residues[:, None]).astype(
        jnp.bfloat16
    )
    added = jnp.dot(picks, table, preferred_element_type=jnp.float32)
    summed = grad_out.astype(jnp.float32) + spots[:, :, None] * added[:, None, :]
    return summed.astype(jnp.bfloat16)


def log_total(scores):
    row_max = jnp.max(scores, axis=(-2, -1), keepdims=True)
    return row_max + jnp.log(jnp.sum(jnp.exp(scores - row_max), axis=(-2, -1), keepdims=True))


def slot_mask(count_group):
    slots = jnp.arange(TILES, dtype=jnp.int32)
    return (slots[None, :] < count_group[:, None])[:, None, None, :, None]


def tile_onehot(tile_group, block_count):
    return (
        tile_group[:, :, None] == jnp.arange(block_count, dtype=jnp.int32)[None, None, :]
    ).astype(jnp.bfloat16)


def pick_tiles(blocks, onehot):
    return jnp.einsum("gtb,bkhd->gtkhd", onehot, blocks, preferred_element_type=jnp.float32).astype(
        jnp.bfloat16
    )


def add_tiles(total, terms, onehot):
    high_part = terms.astype(jnp.bfloat16)
    low_part = (terms - high_part.astype(jnp.float32)).astype(jnp.bfloat16)
    total = total + jnp.einsum(
        "gtb,rgtkhd->rbkhd", onehot, high_part, preferred_element_type=jnp.float32
    )
    return total + jnp.einsum(
        "gtb,rgtkhd->rbkhd", onehot, low_part, preferred_element_type=jnp.float32
    )


def tile_scores(query_group, key_blocks, onehot, live_slots, softmax_scale):
    key_tiles = pick_tiles(key_blocks, onehot)
    scores = (
        jnp.einsum("gqhd,gtkhd->ghqtk", query_group, key_tiles, preferred_element_type=jnp.float32)
        * softmax_scale
    )
    return (jnp.where(live_slots, scores, -1e30), key_tiles)


def block_stats(query_blocks, key_blocks, tiles, counts, first_block, block_total, softmax_scale):
    group = math.gcd(max(1, 512 // BLOCK), block_total)
    block_count = key_blocks.shape[0]

    def group_stats(group_index):
        offset_at = first_block + group_index * group
        query_group = lax.dynamic_slice_in_dim(query_blocks, offset_at, group, 0)
        tile_group = lax.dynamic_slice_in_dim(tiles, offset_at, group, 0)
        count_group = lax.dynamic_slice_in_dim(counts, offset_at, group, 0)
        scores, unused = tile_scores(
            query_group,
            key_blocks,
            tile_onehot(tile_group, block_count),
            slot_mask(count_group),
            softmax_scale,
        )
        return log_total(scores)[..., 0, 0]

    stacked = lax.map(group_stats, jnp.arange(block_total // group, dtype=jnp.int32))
    return stacked.reshape((block_total,) + stacked.shape[2:])


def per_device(queries, keys, values, grad_out, table, positions, residues, tiles, counts):
    tok_count = queries.shape[0]
    row_devices = lax.axis_size("rows")
    softmax_scale = D_HEAD ** (-0.5)
    query_heads, key_heads, value_heads = (
        lax.all_to_all(queries, "seq", split_axis=1, concat_axis=0, tiled=True),
        lax.all_to_all(keys, "seq", split_axis=1, concat_axis=0, tiled=True),
        lax.all_to_all(values, "seq", split_axis=1, concat_axis=0, tiled=True),
    )
    cotangent = substitute(grad_out, table, positions, residues, lax.axis_index("seq") * tok_count)
    cot_heads = lax.all_to_all(cotangent, "seq", split_axis=2, concat_axis=1, tiled=True)
    seq_len = query_heads.shape[0]
    width_local = query_heads.shape[1]
    heads_local = width_local // D_HEAD
    block_count = seq_len // BLOCK
    row_count = cot_heads.shape[0]
    block_shape = (block_count, BLOCK, heads_local, D_HEAD)
    query_blocks = query_heads.reshape(block_shape)
    key_blocks = key_heads.reshape(block_shape)
    value_blocks = value_heads.reshape(block_shape)
    cot_blocks = cot_heads.reshape((row_count,) + block_shape)
    share_count = block_count // row_devices
    own_stats = block_stats(
        query_blocks,
        key_blocks,
        tiles,
        counts,
        lax.axis_index("rows") * share_count,
        share_count,
        softmax_scale,
    )
    log_totals = lax.all_gather(own_stats, "rows", axis=0, tiled=True)
    group = math.gcd(max(1, 512 // BLOCK), block_count)

    def step(totals, group_index):
        grad_query, grad_keys, grad_values = totals
        offset_at = group_index * group
        query_group = lax.dynamic_slice_in_dim(query_blocks, offset_at, group, 0)
        tile_group = lax.dynamic_slice_in_dim(tiles, offset_at, group, 0)
        count_group = lax.dynamic_slice_in_dim(counts, offset_at, group, 0)
        stats_group = lax.dynamic_slice_in_dim(log_totals, offset_at, group, 0)
        cot_group = lax.dynamic_slice_in_dim(cot_blocks, offset_at, group, 1)
        live_slots = slot_mask(count_group)
        onehot = tile_onehot(tile_group, block_count)
        scores, key_tiles = tile_scores(query_group, key_blocks, onehot, live_slots, softmax_scale)
        value_tiles = pick_tiles(value_blocks, onehot)
        probs = jnp.where(live_slots, jnp.exp(scores - stats_group[:, :, :, None, None]), 0.0)
        probs_bf = probs.astype(jnp.bfloat16)
        grad_probs = jnp.einsum(
            "rgqhd,gtkhd->rghqtk", cot_group, value_tiles, preferred_element_type=jnp.float32
        )
        delta = jnp.sum(probs[None] * grad_probs, axis=(4, 5), keepdims=True)
        grad_scores = (probs[None] * (grad_probs - delta)).astype(jnp.bfloat16)
        query_terms = (
            softmax_scale
            * jnp.einsum(
                "rghqtk,gtkhd->rgqhd", grad_scores, key_tiles, preferred_element_type=jnp.float32
            )
        ).astype(jnp.bfloat16)
        key_terms = softmax_scale * jnp.einsum(
            "rghqtk,gqhd->rgtkhd", grad_scores, query_group, preferred_element_type=jnp.float32
        )
        value_terms = jnp.einsum(
            "ghqtk,rgqhd->rgtkhd", probs_bf, cot_group, preferred_element_type=jnp.float32
        )
        grad_keys = add_tiles(grad_keys, key_terms, onehot)
        grad_values = add_tiles(grad_values, value_terms, onehot)
        grad_query = lax.dynamic_update_slice_in_dim(grad_query, query_terms, offset_at, 1)
        return ((grad_query, grad_keys, grad_values), None)

    zeros_full = jnp.zeros((row_count,) + block_shape, jnp.float32)
    initial = (jnp.zeros((row_count,) + block_shape, jnp.bfloat16), zeros_full, zeros_full)
    finals, unused = lax.scan(step, initial, jnp.arange(block_count // group, dtype=jnp.int32))
    grad_query, grad_keys, grad_values = finals
    flat_shape = (row_count, seq_len, width_local)
    return (
        lax.all_to_all(
            grad_query.reshape(flat_shape), "seq", split_axis=1, concat_axis=2, tiled=True
        ),
        lax.all_to_all(
            grad_keys.reshape(flat_shape).astype(jnp.bfloat16),
            "seq",
            split_axis=1,
            concat_axis=2,
            tiled=True,
        ),
        lax.all_to_all(
            grad_values.reshape(flat_shape).astype(jnp.bfloat16),
            "seq",
            split_axis=1,
            concat_axis=2,
            tiled=True,
        ),
    )


def solution(mesh):
    placed = (
        P("seq", None),
        P("seq", None),
        P("seq", None),
        P("rows", "seq", None),
        P(),
        P("rows"),
        P("rows"),
        P(),
        P(),
    )
    return jax.shard_map(
        per_device,
        mesh=mesh,
        in_specs=placed,
        out_specs=(P("rows", "seq", None), P("rows", "seq", None), P("rows", "seq", None)),
        check_vma=False,
    )
```

profile of v0, /device:TPU:2, one launch (start us, length us, event | category | flops | bytes accessed | tf_op | source)
XLA Modules:
  0.0 763.2 jit_solution(254725159032341387)
XLA Ops:
  4.5 7.3 copy.236
  12.3 21.6 %reduce.1 = bf16[4096,256]{1,0:T(8,128)(2,1)S(1)} reduce(bf16[4096,1,256]{2,1,0:T(2,128)(2,1)} %bitcast.296, bf16[]{:T(256)} %broadcast.138), dimensions={1}, to_apply=%bitcast.195.reduce_sub_computation | reduce | bytes 4194306
  35.9 7.5 all-to-all-start.3
  47.4 23.1 %all-to-all-done.3 = bf16[16,2,32768]{2,1,0:T(2,128)(2,1)S(1)} async-done(((bf16[16,2,32768]{2,1,0:T(2,128)(2,1)}), bf16[16,2,32768]{2,1,0:T(2,128)(2,1)S(1)}, u32[]{:S(2)}, u32[]{:S(2)}) %all-to-all-start.3) | async-done | bytes 2097184 | tf_op jit(solution)/shard_map/all_to_all | solution.py:99
  70.5 7.5 all-to-all-start.1
  82.1 21.1 %all-to-all-done.1 = bf16[256,16,256]{0,2,1:T(8,128)(2,1)} async-done(((bf16[256,16,256]{0,2,1:T(8,128)(2,1)}), bf16[256,16,256]{0,2,1:T(8,128)(2,1)}, u32[]{:S(2)}, u32[]{:S(2)}) %all-to-all-start.1) | async-done | bytes 2097184 | tf_op jit(solution)/shard_map/all_to_all | solution.py:94
  103.2 7.1 all-to-all-start
  114.4 21.0 %all-to-all-done = bf16[256,16,256]{0,2,1:T(8,128)(2,1)} async-done(((bf16[256,16,256]{0,2,1:T(8,128)(2,1)}), bf16[256,16,256]{0,2,1:T(8,128)(2,1)}, u32[]{:S(2)}, u32[]{:S(2)}) %all-to-all-start) | async-done | bytes 2097184 | tf_op jit(solution)/shard_map/all_to_all | solution.py:95
  135.4 7.7 %all-to-all-start.2 = ((bf16[256,16,256]{0,2,1:T(8,128)(2,1)}), bf16[256,16,256]{0,2,1:T(8,128)(2,1)}, u32[]{:S(2)}, u32[]{:S(2)}) async-start(bf16[256,16,256]{0,2,1:T(8,128)(2,1)} %bitcast.309), calls=%async_computation.2 | async-start | bytes 4194304 | tf_op jit(solution)/shard_map/all_to_all | solution.py:96
  143.5 6.7 reshape.258
  194.2 14.1 %all_gather.3 = f32[32,2,128]{2,1,0:T(2,128)S(1)} all-gather(f32[4,2,128]{2,1,0:T(2,128)S(1)} %bitcast.317), channel_id=1, replica_groups=mesh['rows'=8,'seq'=16] {'rows'}, dimensions={0}, use_global_device_ids=true | all-gather | bytes 36864 | tf_op jit(solution)/shard_map/all_gather | solution.py:120
  211.5 353.2 %while.5 = (s32[]{:T(128)}, bf16[1,32,128,2,128]{4,3,2,1,0:T(2,128)(2,1)}, f32[1,32,128,2,128]{4,1,3,2,0:T(8,128)}, f32[1,32,128,2,128]{4,1,3,2,0:T(8,128)}, s32...) while((s32[]{:T(128)}, ...), condition=%wide.region_4.5_spmd.clone, body=%wide.region_2.0_spmd.clone.sunk | while | flops 1784943616 | bytes 221541968 | solution.py:161
  569.7 6.2 reshape.256
  575.9 21.6 %reduce.4 = bf16[4096,256]{1,0:T(8,128)(2,1)S(1)} reduce(bf16[4096,1,256]{2,1,0:T(2,128)(2,1)} %bitcast.299, bf16[]{:T(256)} %broadcast.138), dimensions={1}, to_apply=%bitcast.201.reduce_sub_computation | reduce | bytes 4194306
  599.5 7.3 all-to-all-start.6
  613.0 13.5 %reshape.255 = bf16[1,4096,256]{2,0,1:T(2,128)(2,1)} reshape(bf16[1,32,128,2,128]{4,3,2,1,0:T(2,128)(2,1)} %copy.270) | data formatting | bytes 4194304 | tf_op jit(solution)/shard_map/convert_element_type | solution.py:169
  626.5 22.9 %reduce.3 = bf16[4096,256]{1,0:T(8,128)(2,1)} reduce(bf16[4096,1,256]{2,1,0:T(2,128)(2,1)} %bitcast.300, bf16[]{:T(256)} %broadcast.138), dimensions={1}, to_apply=%bitcast.199.reduce_sub_computation | reduce | bytes 4194306
  653.3 7.5 all-to-all-start.5
  660.9 13.5 %reshape.254 = bf16[1,4096,256]{2,0,1:T(2,128)(2,1)} reshape(bf16[1,32,128,2,128]{4,3,2,1,0:T(2,128)(2,1)} %get-tuple-element.88) | data formatting | bytes 4194304 | tf_op jit(solution)/shard_map/reshape | solution.py:166
  674.4 22.9 %reduce.2 = bf16[4096,256]{1,0:T(8,128)(2,1)} reduce(bf16[4096,1,256]{2,1,0:T(2,128)(2,1)} %bitcast.297, bf16[]{:T(256)} %broadcast.138), dimensions={1}, to_apply=%bitcast.197.reduce_sub_computation | reduce | bytes 4194306
  701.2 7.2 all-to-all-start.4
  708.5 6.7 reshape.264
  724.1 10.4 %reshape.262 = bf16[4096,1,256]{2,1,0:T(2,128)(2,1)} reshape(bf16[16,2,32768]{2,1,0:T(2,128)(2,1)} %all-to-all-done.5) | data formatting | bytes 4194304
  743.5 10.4 %reshape.260 = bf16[4096,1,256]{2,1,0:T(2,128)(2,1)} reshape(bf16[16,2,32768]{2,1,0:T(2,128)(2,1)} %all-to-all-done.4) | data formatting | bytes 4194304
  (366 shorter events, 447.2 us)
Async XLA Ops:
  35.9 34.6 %all-to-all-start.3 = ((bf16[16,2,32768]{2,1,0:T(2,128)(2,1)}), bf16[16,2,32768]{2,1,0:T(2,128)(2,1)S(1)}, u32[]{:S(2)}, u32[]{:S(2)}) async-start(bf16[16,2,32768]{2,1,0:T(2,128)(2,1)} %reshape.257), calls=%async_computation.3 | async-start | bytes 4194304 | tf_op jit(solution)/shard_map/all_to_all | solution.py:99
  70.5 32.7 %all-to-all-start.1 = ((bf16[256,16,256]{0,2,1:T(8,128)(2,1)}), bf16[256,16,256]{0,2,1:T(8,128)(2,1)}, u32[]{:S(2)}, u32[]{:S(2)}) async-start(bf16[256,16,256]{0,2,1:T(8,128)(2,1)} %bitcast.310), calls=%async_computation.1 | async-start | bytes 4194304 | tf_op jit(solution)/shard_map/all_to_all | solution.py:94
  103.2 32.2 %all-to-all-start = ((bf16[256,16,256]{0,2,1:T(8,128)(2,1)}), bf16[256,16,256]{0,2,1:T(8,128)(2,1)}, u32[]{:S(2)}, u32[]{:S(2)}) async-start(bf16[256,16,256]{0,2,1:T(8,128)(2,1)} %bitcast.311), calls=%async_computation | async-start | bytes 4194304 | tf_op jit(solution)/shard_map/all_to_all | solution.py:95
  135.4 7.8 %copy-start.7 = (s32[32,8]{0,1:T(8,128)S(1)}, s32[32,8]{0,1:T(8,128)}, u32[]{:S(2)}) copy-start(s32[32,8]{0,1:T(8,128)} %param.18) | copy-start | bytes 3076
  135.4 7.8 %copy-start.8 = (s32[32]{0:T(128)S(1)}, s32[32]{0:T(128)}, u32[]{:S(2)}) copy-start(s32[32]{0:T(128)} %param.19) | copy-start | bytes 388
  135.4 42.8 %all-to-all-start.2 = ((bf16[256,16,256]{0,2,1:T(8,128)(2,1)}), bf16[256,16,256]{0,2,1:T(8,128)(2,1)}, u32[]{:S(2)}, u32[]{:S(2)}) async-start(bf16[256,16,256]{0,2,1:T(8,128)(2,1)} %bitcast.309), calls=%async_computation.2 | async-start | bytes 4194304 | tf_op jit(solution)/shard_map/all_to_all | solution.py:96
  247.5 2.9 copy-start.2
  259.9 2.8 copy-start.3
  290.1 2.9 copy-start.2
  302.5 2.8 copy-start.3
  332.7 2.9 copy-start.2
  375.3 2.9 copy-start.2
  387.7 2.8 copy-start.3
  417.9 2.9 copy-start.2
  430.3 2.8 copy-start.3
  460.5 2.9 copy-start.2
  503.1 2.9 copy-start.2
  515.5 2.8 copy-start.3
  545.7 2.9 copy-start.2
  558.1 2.8 copy-start.3
  599.5 53.9 %all-to-all-start.6 = ((bf16[16,2,32768]{2,1,0:T(2,128)(2,1)}), bf16[16,2,32768]{2,1,0:T(2,128)(2,1)S(1)}, u32[]{:S(2)}, u32[]{:S(2)}) async-start(bf16[16,2,32768]{2,1,0:T(2,128)(2,1)} %reshape.263), calls=%async_computation.6 | async-start | bytes 4194304 | tf_op jit(solution)/shard_map/all_to_all | solution.py:175
  653.3 47.9 %all-to-all-start.5 = ((bf16[16,2,32768]{2,1,0:T(2,128)(2,1)}), bf16[16,2,32768]{2,1,0:T(2,128)(2,1)}, u32[]{:S(2)}, u32[]{:S(2)}) async-start(bf16[16,2,32768]{2,1,0:T(2,128)(2,1)} %reshape.261), calls=%async_computation.5 | async-start | bytes 4194304 | tf_op jit(solution)/shard_map/all_to_all | solution.py:168
  701.2 42.3 %all-to-all-start.4 = ((bf16[16,2,32768]{2,1,0:T(2,128)(2,1)}), bf16[16,2,32768]{2,1,0:T(2,128)(2,1)}, u32[]{:S(2)}, u32[]{:S(2)}) async-start(bf16[16,2,32768]{2,1,0:T(2,128)(2,1)} %reshape.259), calls=%async_computation.4 | async-start | bytes 4194304 | tf_op jit(solution)/shard_map/all_to_all | solution.py:165
  758.9 4.1 copy-start.1
  (27 other events, 60.9 us)
where the time goes:
time: 773 us; the launch traced here: 763 us
  local copies, waits for them, and re-layouts  281 us (36%)
  matrix products  188 us (24%)
  other arithmetic  142 us (18%)
  waiting for transfers between devices  65.2 us (8%)
  starting transfers between devices  51.9 us (7%)
  loops' own time  18.8 us (2%)
  blocking collectives  14.1 us (2%)
    unnamed x31, local copies, waits for them, and re-layouts  95.8 us
    unnamed x6, other arithmetic  88.9 us
    another operation x16, local copies, waits for them, and re-layouts  52.3 us
    another operation x40, other arithmetic  43.5 us
    dot_general x17, matrix products, pick_tiles(): jnp.einsum('gtb,bkhd->gtkhd', onehot, blocks, preferred_element_type=jnp....  39.9 us
    dot_general x16, matrix products, add_tiles(): jnp.einsum('gtb,rgtkhd->rbkhd', onehot, low_part, preferred_element_type=...  34.5 us
    dot_general x16, matrix products, add_tiles(): jnp.einsum('gtb,rgtkhd->rbkhd', onehot, high_part, preferred_element_type...  33.9 us
    dot_general x8, matrix products, step(): jnp.einsum('ghqtk,rgqhd->rgtkhd', probs_bf, cot_group, preferred_element_...  25.2 us
  transfers between devices with their start and end apart: 7, of which 3 were waited for; matrix products, arithmetic and copies ran while one was open for 22% of the time, Pallas kernels for 0%

commit v1 on v0

--- a/solution.py
+++ b/solution.py
@@ -96,7 +96,10 @@
         lax.all_to_all(values, "seq", split_axis=1, concat_axis=0, tiled=True),
     )
     cotangent = substitute(grad_out, table, positions, residues, lax.axis_index("seq") * tok_count)
-    cot_heads = lax.all_to_all(cotangent, "seq", split_axis=2, concat_axis=1, tiled=True)
+    size = lax.axis_size("seq")
+    parts = jnp.stack(jnp.split(cotangent, size, axis=2), axis=0)
+    parts = lax.all_to_all(parts, "seq", split_axis=0, concat_axis=0)
+    cot_heads = jnp.concatenate(parts, axis=1)
     seq_len = query_heads.shape[0]
     width_local = query_heads.shape[1]
     heads_local = width_local // D_HEAD

time: 773 us -> 718 us (0.929)
  other arithmetic: 142 us -> 120 us
  loops' own time: 18.8 us -> 6.85 us
  waiting for transfers between devices: 65.2 us -> 54.8 us
  local copies, waits for them, and re-layouts: 281 us -> 272 us
    all_to_all x1, waiting for transfers between devices: 23.1 us -> 0.01 us  [per_device(): parts = lax.all_to_all(parts, 'seq', split_axis=0, concat_axis=0)]
    unnamed x6 -> x5, other arithmetic: 88.9 us -> 67.5 us
    all_to_all x1, waiting for transfers between devices: 0.01 us -> 19.1 us  [per_device(): lax.all_to_all(values, 'seq', split_axis=1, concat_axis=0, tiled=True)]
    another operation x1, loops' own time: 18.8 us -> 6.85 us  [per_device(): lax.scan(step, initial, jnp.arange(block_count // group, dtype=jnp.int32))]
    another operation x16 -> x18, local copies, waits for them, and re-layouts: 52.3 us -> 56.6 us
    unnamed x31 -> x47, local copies, waits for them, and re-layouts: 95.8 us -> 94.7 us
  transfers between devices with their start and end apart: 7 -> 7, of which waited for: 3 -> 3; matrix products, arithmetic and copies ran while one was open for 22% -> 25% of each run, Pallas kernels for 0% -> 0%
where the time goes in v1:
time: 718 us; the launch traced here: 710 us
  local copies, waits for them, and re-layouts  272 us (38%)
  matrix products  188 us (26%)
  other arithmetic  120 us (17%)
  waiting for transfers between devices  54.8 us (8%)
  starting transfers between devices  51.9 us (7%)
  blocking collectives  14.1 us (2%)
    unnamed x47, local copies, waits for them, and re-layouts  94.7 us
    unnamed x5, other arithmetic  67.5 us
    another operation x16, local copies, waits for them, and re-layouts  52 us
    another operation x40, other arithmetic  43.3 us
    dot_general x17, matrix products, pick_tiles(): jnp.einsum('gtb,bkhd->gtkhd', onehot, blocks, preferred_element_type=jnp....  39.7 us
    dot_general x16, matrix products, add_tiles(): jnp.einsum('gtb,rgtkhd->rbkhd', onehot, low_part, preferred_element_type=...  34.5 us
    dot_general x16, matrix products, add_tiles(): jnp.einsum('gtb,rgtkhd->rbkhd', onehot, high_part, preferred_element_type...  33.8 us
    dot_general x8, matrix products, step(): jnp.einsum('ghqtk,rgqhd->rgtkhd', probs_bf, cot_group, preferred_element_...  25 us
  transfers between devices with their start and end apart: 7, of which 3 were waited for; matrix products, arithmetic and copies ran while one was open for 25% of the time, Pallas kernels for 0%

profile of v1, /device:TPU:2, one launch (start us, length us, event | category | flops | bytes accessed | tf_op | source)
XLA Modules:
  0.0 709.6 jit_solution(17822086281596393366)
XLA Ops:
  0.6 4.1 copy.144
  4.8 7.5 %all-to-all-start.1 = ((bf16[256,16,256]{0,2,1:T(8,128)(2,1)}), bf16[256,16,256]{0,2,1:T(8,128)(2,1)S(1)}, u32[]{:S(2)}, u32[]{:S(2)}) async-start(bf16[256,16,256]{0,2,1:T(8,128)(2,1)} %bitcast.365), calls=%async_computation.1 | async-start | bytes 4194304 | tf_op jit(solution)/shard_map/all_to_all | solution.py:94
  17.8 21.6 %all-to-all-done.1 = bf16[256,16,256]{0,2,1:T(8,128)(2,1)S(1)} async-done(((bf16[256,16,256]{0,2,1:T(8,128)(2,1)}), bf16[256,16,256]{0,2,1:T(8,128)(2,1)S(1)}, u32[]{:S(2)}, u32[]{:S(2)}) %all-to-all-start.1) | async-done | bytes 2097184 | tf_op jit(solution)/shard_map/all_to_all | solution.py:94
  40.7 7.5 %all-to-all-start = ((bf16[256,16,256]{0,2,1:T(8,128)(2,1)}), bf16[256,16,256]{0,2,1:T(8,128)(2,1)}, u32[]{:S(2)}, u32[]{:S(2)}) async-start(bf16[256,16,256]{0,2,1:T(8,128)(2,1)} %bitcast.364), calls=%async_computation | async-start | bytes 4194304 | tf_op jit(solution)/shard_map/all_to_all | solution.py:95
  59.3 14.1 %all-to-all-done = bf16[256,16,256]{0,2,1:T(8,128)(2,1)} async-done(((bf16[256,16,256]{0,2,1:T(8,128)(2,1)}), bf16[256,16,256]{0,2,1:T(8,128)(2,1)}, u32[]{:S(2)}, u32[]{:S(2)}) %all-to-all-start) | async-done | bytes 2097184 | tf_op jit(solution)/shard_map/all_to_all | solution.py:95
  73.4 7.1 all-to-all-start.2
  86.5 19.1 %all-to-all-done.2 = bf16[256,16,256]{0,2,1:T(8,128)(2,1)} async-done(((bf16[256,16,256]{0,2,1:T(8,128)(2,1)}), bf16[256,16,256]{0,2,1:T(8,128)(2,1)}, u32[]{:S(2)}, u32[]{:S(2)}) %all-to-all-start.2) | async-done | bytes 2097184 | tf_op jit(solution)/shard_map/all_to_all | solution.py:96
  105.6 7.8 %all-to-all-start.3 = ((bf16[16,1,256,256]{3,2,1,0:T(8,128)(2,1)}), bf16[16,1,256,256]{3,2,1,0:T(8,128)(2,1)}, u32[]{:S(2)}, u32[]{:S(2)}) async-start(bf16[16,1,256,256]{3,2,1,0:T(8,128)(2,1)} %fusion.83), calls=%async_computation.3 | async-start | bytes 4194304 | tf_op jit(solution)/shard_map/all_to_all | solution.py:101
  126.6 5.1 copy.154
  142.7 5.1 copy.156
  150.5 14.1 %all_gather.3 = f32[32,2,128]{2,1,0:T(2,128)S(1)} all-gather(f32[4,2,128]{2,1,0:T(2,128)S(1)} %bitcast.371), channel_id=1, replica_groups=mesh['rows'=8,'seq'=16] {'rows'}, dimensions={0}, use_global_device_ids=true | all-gather | bytes 36864 | tf_op jit(solution)/shard_map/all_gather | solution.py:123
  171.8 338.4 %while.5 = (s32[]{:T(128)}, bf16[1,32,128,2,128]{4,3,2,1,0:T(2,128)(2,1)}, f32[1,32,128,2,128]{4,1,3,2,0:T(8,128)}, f32[1,32,128,2,128]{4,1,3,2,0:T(8,128)}, s32...) while((s32[]{:T(128)}, ...), condition=%wide.region_4.5_spmd.clone, body=%wide.region_2.0_spmd.clone.sunk | while | flops 1784943616 | bytes 221017680 | solution.py:164
  515.2 6.2 reshape.252
  522.0 21.6 %reduce.3 = bf16[4096,256]{1,0:T(8,128)(2,1)S(1)} reduce(bf16[4096,1,256]{2,1,0:T(2,128)(2,1)} %bitcast.352, bf16[]{:T(256)} %broadcast.138), dimensions={1}, to_apply=%bitcast.257.reduce_sub_computation | reduce | bytes 4194306
  545.6 7.3 %all-to-all-start.6 = ((bf16[16,2,32768]{2,1,0:T(2,128)(2,1)}), bf16[16,2,32768]{2,1,0:T(2,128)(2,1)S(1)}, u32[]{:S(2)}, u32[]{:S(2)}) async-start(bf16[16,2,32768]{2,1,0:T(2,128)(2,1)} %reshape.257), calls=%async_computation.6 | async-start | bytes 4194304 | tf_op jit(solution)/shard_map/all_to_all | solution.py:178
  559.1 13.5 %reshape.251 = bf16[1,4096,256]{2,0,1:T(2,128)(2,1)} reshape(bf16[1,32,128,2,128]{4,3,2,1,0:T(2,128)(2,1)} %copy.187) | data formatting | bytes 4194304 | tf_op jit(solution)/shard_map/convert_element_type | solution.py:172
  572.6 22.9 %reduce.2 = bf16[4096,256]{1,0:T(8,128)(2,1)} reduce(bf16[4096,1,256]{2,1,0:T(2,128)(2,1)} %bitcast.354, bf16[]{:T(256)} %broadcast.138), dimensions={1}, to_apply=%bitcast.255.reduce_sub_computation | reduce | bytes 4194306
  599.5 7.5 %all-to-all-start.5 = ((bf16[16,2,32768]{2,1,0:T(2,128)(2,1)}), bf16[16,2,32768]{2,1,0:T(2,128)(2,1)}, u32[]{:S(2)}, u32[]{:S(2)}) async-start(bf16[16,2,32768]{2,1,0:T(2,128)(2,1)} %reshape.255), calls=%async_computation.5 | async-start | bytes 4194304 | tf_op jit(solution)/shard_map/all_to_all | solution.py:171
  607.1 13.5 %reshape.250 = bf16[1,4096,256]{2,0,1:T(2,128)(2,1)} reshape(bf16[1,32,128,2,128]{4,3,2,1,0:T(2,128)(2,1)} %get-tuple-element.88) | data formatting | bytes 4194304 | tf_op jit(solution)/shard_map/reshape | solution.py:169
  620.6 22.9 %reduce.1 = bf16[4096,256]{1,0:T(8,128)(2,1)} reduce(bf16[4096,1,256]{2,1,0:T(2,128)(2,1)} %bitcast.353, bf16[]{:T(256)} %broadcast.138), dimensions={1}, to_apply=%bitcast.253.reduce_sub_computation | reduce | bytes 4194306
  647.5 7.2 %all-to-all-start.4 = ((bf16[16,2,32768]{2,1,0:T(2,128)(2,1)}), bf16[16,2,32768]{2,1,0:T(2,128)(2,1)}, u32[]{:S(2)}, u32[]{:S(2)}) async-start(bf16[16,2,32768]{2,1,0:T(2,128)(2,1)} %reshape.253), calls=%async_computation.4 | async-start | bytes 4194304 | tf_op jit(solution)/shard_map/all_to_all | solution.py:168
  654.7 6.8 reshape.258
  670.5 10.5 %reshape.256 = bf16[4096,1,256]{2,1,0:T(2,128)(2,1)} reshape(bf16[16,2,32768]{2,1,0:T(2,128)(2,1)} %all-to-all-done.5) | data formatting | bytes 4194304
  690.0 10.5 %reshape.254 = bf16[4096,1,256]{2,1,0:T(2,128)(2,1)} reshape(bf16[16,2,32768]{2,1,0:T(2,128)(2,1)} %all-to-all-done.4) | data formatting | bytes 4194304
  (372 shorter events, 436.9 us)
Async XLA Ops:
  0.6 17.0 %copy-start = (bf16[33,4096]{1,0:T(8,128)(2,1)S(1)}, bf16[33,4096]{1,0:T(8,128)(2,1)}, u32[]{:S(2)}) copy-start(bf16[33,4096]{1,0:T(8,128)(2,1)} %param.15) | copy-start | bytes 811012
  4.8 34.6 %all-to-all-start.1 = ((bf16[256,16,256]{0,2,1:T(8,128)(2,1)}), bf16[256,16,256]{0,2,1:T(8,128)(2,1)S(1)}, u32[]{:S(2)}, u32[]{:S(2)}) async-start(bf16[256,16,256]{0,2,1:T(8,128)(2,1)} %bitcast.365), calls=%async_computation.1 | async-start | bytes 4194304 | tf_op jit(solution)/shard_map/all_to_all | solution.py:94
  40.7 32.7 %all-to-all-start = ((bf16[256,16,256]{0,2,1:T(8,128)(2,1)}), bf16[256,16,256]{0,2,1:T(8,128)(2,1)}, u32[]{:S(2)}, u32[]{:S(2)}) async-start(bf16[256,16,256]{0,2,1:T(8,128)(2,1)} %bitcast.364), calls=%async_computation | async-start | bytes 4194304 | tf_op jit(solution)/shard_map/all_to_all | solution.py:95
  73.4 32.2 %all-to-all-start.2 = ((bf16[256,16,256]{0,2,1:T(8,128)(2,1)}), bf16[256,16,256]{0,2,1:T(8,128)(2,1)}, u32[]{:S(2)}, u32[]{:S(2)}) async-start(bf16[256,16,256]{0,2,1:T(8,128)(2,1)} %bitcast.363), calls=%async_computation.2 | async-start | bytes 4194304 | tf_op jit(solution)/shard_map/all_to_all | solution.py:96
  86.5 26.9 %copy-start.9 = (s32[32,8]{0,1:T(8,128)S(1)}, s32[32,8]{0,1:T(8,128)}, u32[]{:S(2)}) copy-start(s32[32,8]{0,1:T(8,128)} %param.18) | copy-start | bytes 3076
  86.5 26.9 %copy-start.10 = (s32[32]{0:T(128)S(1)}, s32[32]{0:T(128)}, u32[]{:S(2)}) copy-start(s32[32]{0:T(128)} %param.19) | copy-start | bytes 388
  86.5 27.2 %copy-start.8 = (bf16[256,16,256]{0,2,1:T(8,128)(2,1)S(1)}, bf16[256,16,256]{0,2,1:T(8,128)(2,1)}, u32[]{:S(2)}) copy-start(bf16[256,16,256]{0,2,1:T(8,128)(2,1)} %copy-done.7) | copy-start | bytes 6291460
  105.6 59.0 %all-to-all-start.3 = ((bf16[16,1,256,256]{3,2,1,0:T(8,128)(2,1)}), bf16[16,1,256,256]{3,2,1,0:T(8,128)(2,1)}, u32[]{:S(2)}, u32[]{:S(2)}) async-start(bf16[16,1,256,256]{3,2,1,0:T(8,128)(2,1)} %fusion.83), calls=%async_computation.3 | async-start | bytes 4194304 | tf_op jit(solution)/shard_map/all_to_all | solution.py:101
  195.6 2.9 copy-start.2
  208.0 2.8 copy-start.3
  237.8 2.9 copy-start.2
  250.3 2.8 copy-start.3
  280.1 2.9 copy-start.2
  292.5 2.8 copy-start.3
  322.3 2.9 copy-start.2
  334.7 2.8 copy-start.3
  364.5 2.9 copy-start.2
  406.7 2.9 copy-start.2
  448.9 2.9 copy-start.2
  491.2 2.9 copy-start.2
  545.6 53.9 %all-to-all-start.6 = ((bf16[16,2,32768]{2,1,0:T(2,128)(2,1)}), bf16[16,2,32768]{2,1,0:T(2,128)(2,1)S(1)}, u32[]{:S(2)}, u32[]{:S(2)}) async-start(bf16[16,2,32768]{2,1,0:T(2,128)(2,1)} %reshape.257), calls=%async_computation.6 | async-start | bytes 4194304 | tf_op jit(solution)/shard_map/all_to_all | solution.py:178
  599.5 48.0 %all-to-all-start.5 = ((bf16[16,2,32768]{2,1,0:T(2,128)(2,1)}), bf16[16,2,32768]{2,1,0:T(2,128)(2,1)}, u32[]{:S(2)}, u32[]{:S(2)}) async-start(bf16[16,2,32768]{2,1,0:T(2,128)(2,1)} %reshape.255), calls=%async_computation.5 | async-start | bytes 4194304 | tf_op jit(solution)/shard_map/all_to_all | solution.py:171
  647.5 42.5 %all-to-all-start.4 = ((bf16[16,2,32768]{2,1,0:T(2,128)(2,1)}), bf16[16,2,32768]{2,1,0:T(2,128)(2,1)}, u32[]{:S(2)}, u32[]{:S(2)}) async-start(bf16[16,2,32768]{2,1,0:T(2,128)(2,1)} %reshape.253), calls=%async_computation.4 | async-start | bytes 4194304 | tf_op jit(solution)/shard_map/all_to_all | solution.py:168
  705.3 4.1 copy-start.1
  (29 other events, 66.9 us)
